TPU v7x, 256 devices: a whole 4x4x8 slice. The times are simulated.
256 devices in a mesh: dp: 16 (over y, x), expert: 16 (over z, core).
Axes of the slice: x: 4, y: 4, z: 8, core: 2. Of those that a mesh axis runs over, the one named last changes fastest.
Arguments:
- tokens: bfloat16 [256, 6144], P('dp'), may hold values from -6 to 6
- w_gate: bfloat16 [6144, 32768], P(None, ('expert', 'dp')), may hold values from -0.078125 to 0.078125
- w_up: bfloat16 [6144, 32768], P(None, ('expert', 'dp')), may hold values from -0.078125 to 0.078125
- basis: bfloat16 [2, 32768, 6144], P(None, ('expert', 'dp')), may hold values from -5 to 5
- routes: int32 [256, 2], replicated, may hold values from 0 to 3, all different within a row; in each aligned block of 16 rows (0 to 15, 16 to 31, ...) at most 9 rows name the same one
- gates: float32 [256, 2], replicated, may hold values from 0.1 to 0.9
- rho: float32 [256], P('dp'), may hold values from 0.3 to 3
- sigma: float32 [6144], replicated, may hold values from 0.3 to 3
Outputs:
- krylov_next: bfloat16 [32768, 6144], P(('expert', 'dp'))
- hessenberg: float32 [3, 1], replicated
Inputs may be any that keep to these rules, and one draw needn't show every extreme that they name: `routes`: in each aligned block of 16 rows (the rows of one index of dp), no expert is named by more than 9 rows; the 2 entries of a row differ.
All inputs are finite; a program needn't handle non-finite values.
Results may differ from a plain program's by a relative error of at most 0.0062.
The roundings to bfloat16 on the way count: a program that leaves them out, or rounds other values in their place, can miss the bound.
Values may be sent and summed in bfloat16 or wider, within the bound.
A program may use at most 64 MiB of HBM per device.

v0:
```python
import functools
import math

import jax
import jax.numpy as jnp
from jax import lax
from jax.experimental import pallas as pl
from jax.experimental.pallas import tpu as pltpu
from jax.sharding import Mesh
from jax.sharding import PartitionSpec as P

D = 6144
FF = 8192
E = 4
HALF = 3072
GROUP = 768
SIDE = 128
MSG = HALF + SIDE + 512
ROWS = 144
CHUNK = 216
DP = ("dp_0", "dp_1")
EXPERT = ("expert_0", "expert_1")
EXPERT_DP = ("expert_0", "expert_1", "dp_0", "dp_1")
AXES = ("dp_0", "dp_1", "expert_0", "expert_1")
MESH = pl.DeviceIdType.MESH
F32 = jnp.float32
BF16 = jnp.bfloat16
SCALE = 1.0 / math.sqrt(FF)
KAPPA = E * FF / 256
ENTRIES = float(E * FF * D)
OFFSETS = (1, 3, 2)


def iota(shape, dim):
    return lax.broadcasted_iota(jnp.int32, shape, dim)


def parts(col):
    hi = col.astype(BF16)
    left = col - hi.astype(F32)
    mid = left.astype(BF16)
    low = (left - mid.astype(F32)).astype(BF16)
    return hi.astype(F32), mid.astype(F32), low.astype(F32)


def joined(side, first):
    return (side[:, first : first + 1] + side[:, first + 1 : first + 2]) + side[:, first + 2 : first + 3]


def slot_order(m):
    return jnp.concatenate([m[0:64], m[128:136], m[64:128], m[136:144]], axis=0)


def kernel(
    tok_hbm, wg_hbm, wu_hbm, basis_hbm, routes_hbm, gates_hbm, rho_hbm, sigma_hbm,
    out, hess,
    routes, gates, rho, sigma, cols, tokv, wbuf, v0, v1, v0x, v1x, gm, gd, exf, exs, side_main, pre_s, pre_r, hid, hid_t,
    tb, r1, town, p2s, r2, zs, rz0, zes, rz, amat, amat_h, rank_s, rho_s, c4, cx, cg, img,
    red_a, red_b, red_s,
    loc_sem, core_send, core_recv, ag_send, ag_recv, rs_send, rs_recv, z_send, z_recv,
    cg_send, cg_recv, cx_send, cx_recv, ra_send, ra_recv, rb_send, rb_recv,
):
    y, x, z, c = [lax.axis_index(name) for name in AXES]
    a1 = y * (1 - c) + x * c
    a2 = x * (1 - c) + y * c
    p = y * 4 + x
    q = z * 2 + c
    e = z // 2

    def plane(b1, b2):
        return (b1 * (1 - c) + b2 * c, b2 * (1 - c) + b1 * c, z, c)

    def send(src, dst, s_sem, r_sem, device):
        copy = pltpu.make_async_remote_copy(
            src_ref=src, dst_ref=dst, send_sem=s_sem, recv_sem=r_sem, device_id=device, device_id_type=MESH
        )
        copy.start()
        return copy

    def local(src, dst, sem):
        copy = pltpu.make_async_copy(src, dst, sem)
        copy.start()
        return copy

    mine = pl.ds(pl.multiple_of(c * HALF, HALF), HALF)
    other = pl.ds(pl.multiple_of((1 - c) * HALF, HALF), HALF)
    small = [
        local(routes_hbm, routes, loc_sem.at[7]),
        local(gates_hbm, gates, loc_sem.at[8]),
        local(rho_hbm, rho, loc_sem.at[9]),
    ]
    loads = [
        local(tok_hbm.at[:, mine], tokv, loc_sem.at[0]),
        local(wg_hbm.at[mine, :], wbuf.at[0, :, pl.ds(0, 128)], loc_sem.at[1]),
        local(wu_hbm.at[mine, :], wbuf.at[0, :, pl.ds(128, 128)], loc_sem.at[2]),
        local(basis_hbm.at[1, :, mine], v1.at[0], loc_sem.at[3]),
        local(basis_hbm.at[0, :, mine], v0.at[0], loc_sem.at[4]),
        local(basis_hbm.at[1, :, other], v1x, loc_sem.at[5]),
        local(basis_hbm.at[0, :, other], v0x, loc_sem.at[6]),
        local(sigma_hbm, sigma, loc_sem.at[10]),
    ]
    barrier = pltpu.get_barrier_semaphore()
    for k in range(1, 16):
        o = (p + k) % 16
        pl.semaphore_signal(barrier, inc=1, device_id=(o // 4, o % 4, z, c), device_id_type=MESH)
        o = (q + k) % 16
        pl.semaphore_signal(barrier, inc=1, device_id=(y, x, o // 2, o % 2), device_id_type=MESH)

    for copy in small:
        copy.wait()

    cols[...] = jnp.transpose(
        jnp.concatenate([routes[...].astype(F32), gates[...], jnp.zeros((4, 256), F32)], axis=0)
    )
    own = cols[pl.ds(pl.multiple_of(p * 16, 16), 16), :]
    ef = e.astype(F32)
    hit0 = own[:, 0:1] == ef
    hit1 = own[:, 1:2] == ef
    member = hit0.astype(F32) + hit1.astype(F32)
    gate_tok = jnp.where(hit0, own[:, 2:3], 0.0) + jnp.where(hit1, own[:, 3:4], 0.0)
    tri = (iota((16, 16), 1) <= iota((16, 16), 0)).astype(F32).astype(BF16)
    member_b = jnp.broadcast_to(member, (16, 128))
    rank = jnp.dot(tri, member_b.astype(BF16), preferred_element_type=F32)
    lane = iota((16, 128), 1)
    place_t = jnp.where((rank - 1.0 == lane.astype(F32)) & (member_b > 0), 1.0, 0.0)
    place = jnp.transpose(place_t)[0:16, :].astype(BF16)
    diagonal = iota((16, 16), 0) == iota((16, 16), 1)
    rho_tok = jnp.sum(jnp.where(diagonal, jnp.broadcast_to(rho[...], (16, 16)), 0.0), axis=1, keepdims=True)
    r_hi, r_mid, r_low = parts(rho_tok)
    g_hi, g_mid, g_low = parts(gate_tok)
    side_in = jnp.zeros((16, 128), F32)
    for index, col in enumerate((r_hi, r_mid, r_low, g_hi, g_mid, g_low)):
        side_in = jnp.where(lane == index, col, side_in)
    side = jnp.dot(place, side_in.astype(BF16), preferred_element_type=F32)
    m = a1 * 4 + a2
    gm[m, :, HALF : HALF + SIDE] = side[0:8].astype(BF16)
    gm[m, :, HALF + SIDE + 384 : MSG] = jnp.broadcast_to(side[8:9], (8, 128)).astype(BF16)
    loads[0].wait()
    picked = jnp.dot(place, tokv[...], preferred_element_type=F32)
    gm[m, :, 0:HALF] = picked[0:8].astype(BF16)
    for r in range(8):
        exs[r : r + 1, :] = picked[8:9, r * 384 : (r + 1) * 384]
    gm[m, :, HALF + SIDE : HALF + SIDE + 384] = exs[...].astype(BF16)

    pl.semaphore_wait(barrier, 30)

    def spread(ref, index, lap, s_sem, r_sem):
        return [
            send(ref.at[index], ref.at[index], s_sem.at[lap, d - 1], r_sem.at[lap, d - 1], plane((a1 + d) % 4, a2))
            for d in OFFSETS
        ]

    def along(ref, s_sem, r_sem):
        return [
            send(ref.at[m], ref.at[m], s_sem.at[4, d - 1], r_sem.at[4, d - 1], plane(a1, (a2 + d) % 4))
            for d in OFFSETS
        ]

    def behind(d):
        return a1 * 4 + (a2 + 4 - d) % 4

    first = along(gm, ag_send, ag_recv)
    second = spread(gm, m, 0, ag_send, ag_recv)
    partner = (y, x, z, 1 - c)
    core = [
        send(wg_hbm.at[other, :], wbuf.at[1, :, pl.ds(0, 128)], core_send.at[0], core_recv.at[0], partner),
        send(wu_hbm.at[other, :], wbuf.at[1, :, pl.ds(128, 128)], core_send.at[1], core_recv.at[1], partner),
        send(basis_hbm.at[1, :, other], v1.at[1], core_send.at[2], core_recv.at[2], partner),
        send(basis_hbm.at[0, :, other], v0.at[1], core_send.at[3], core_recv.at[3], partner),
    ]

    sg = 2 * (z % 2) - 1
    t_lane = iota((256, 128), 1)
    shift = jnp.where(t_lane == 1, sg, 0) + jnp.where(t_lane == 2, -sg, 0) + jnp.where(t_lane == 3, 2, 0)
    names = jnp.where(t_lane < 4, (e + shift + 4) & 3, -1)
    names = names.astype(F32)
    member4 = (cols[:, 0:1] == names).astype(F32) + (cols[:, 1:2] == names).astype(F32)
    low = iota((256, 256), 0)
    col = iota((256, 256), 1)
    tri_b = ((col <= low) & ((col >> 4) == (low >> 4))).astype(F32).astype(BF16)
    rank4 = jnp.dot(tri_b, member4.astype(BF16), preferred_element_type=F32)
    token = iota((256, 128), 0)
    block = token >> 4
    slot = rank4.astype(jnp.int32) - 1
    where_to = (block >> 3) * 72 + jnp.where(slot < 8, (block & 7) * 8 + slot, 64 + (block & 7))
    where_to = jnp.where(member4 > 0, where_to, -1000)
    onehot = (where_to[:, 0:1] == col).astype(F32)
    rank_s[...] = jnp.transpose(onehot)
    h = a2 % 2
    half_rows = pl.ds(pl.multiple_of(h * 72, 8), 72)
    own_full = rank_s[0:ROWS, :].astype(BF16)
    own_half = rank_s[half_rows, :].astype(BF16)
    for k in range(3):
        theirs = (where_to[:, k + 1 : k + 2] == col).astype(F32).astype(BF16)
        amat[k] = jnp.dot(own_full, theirs, preferred_element_type=F32)[:, 0:ROWS].astype(BF16)
        theirs = (where_to[:, k + 1 : k + 2] - h * 72 == col).astype(F32).astype(BF16)
        amat_h[k] = jnp.dot(own_half, theirs, preferred_element_type=F32)[:, 0:72].astype(BF16)

    for d, copy in zip(OFFSETS, first):
        copy.wait_recv()
        second += spread(gm, behind(d), d, ag_send, ag_recv)

    for copy in loads[1:]:
        copy.wait()
    for copy in core[2:]:
        copy.wait_recv()

    def gram(k, sums):
        s00, s01, s11 = sums
        part = pl.ds(pl.multiple_of(k * 256, 256), 256)
        for u in range(2):
            b0 = v0[u, :, part].astype(F32)
            b1 = v1[u, :, part].astype(F32)
            fold = lambda a: jnp.sum(a.reshape(16, 8, 256), axis=0)
            s00 = s00 + fold(b0 * b0)
            s01 = s01 + fold(b0 * b1)
            s11 = s11 + fold(b1 * b1)
        return s00, s01, s11

    zero = jnp.zeros((8, 256), F32)
    s00, s01, s11 = lax.fori_loop(0, HALF // 256, gram, (zero, zero, zero))

    for copy in second:
        copy.wait_recv()
    for copy in core[:2]:
        copy.wait_recv()

    def source(o):
        return o * (1 - c) + ((o % 4) * 4 + o // 4) * c

    for k in range(8):
        pair = [gm[source(2 * k + u), :, 0:HALF].astype(F32) for u in range(2)]
        gd[16 * k : 16 * k + 16, :] = jnp.concatenate(pair, axis=0).astype(BF16)
    for o in range(16):
        block_o = gm[source(o)][:, HALF:MSG].astype(F32)
        side_main[8 * o : 8 * o + 8, :] = block_o[:, 0:SIDE]
        for t in range(4):
            exf[t, 8 * o : 8 * o + 8, :] = block_o[:, SIDE + t * 128 : SIDE + (t + 1) * 128]
    for r in range(8):
        for t in range(3):
            f = r * 384 + t * 128
            gd[128:144, f : f + 128] = exf[t, pl.ds(r, 16, stride=8), :].astype(BF16)
    side_main[128:144, :] = exf[3, pl.ds(0, 16, stride=8), :]

    for u in range(2):
        pre_s[u] = jnp.dot(gd[...], wbuf[u], preferred_element_type=F32)
    pre_copy = send(pre_s, pre_r, core_send.at[4], core_recv.at[4], partner)
    side_all = side_main[...]
    rho_slot = slot_order(jnp.broadcast_to(joined(side_all, 0), (ROWS, 128)))
    rho_s[...] = KAPPA * rho_slot
    gate_slot = slot_order(jnp.broadcast_to(joined(side_all, 3), (ROWS, 128)))
    pre_copy.wait_recv()
    hidden = []
    for u in range(2):
        both = slot_order(pre_s[u] + pre_r[1 - u])
        gate, up = both[:, 0:128], both[:, 128:256]
        hidden.append(gate / (1.0 + jnp.exp(-gate)) * up * gate_slot)
    hidden = jnp.concatenate(hidden, axis=1)
    hid[...] = hidden.astype(BF16)

    rs1 = {}
    for d in OFFSETS + (0,):
        g = (a1 + d) % 4
        part = pl.ds(pl.multiple_of(g * GROUP, GROUP), GROUP)
        rows = v1[:, :, part].reshape(256, GROUP)
        tangent = jnp.dot(hid[...], rows, preferred_element_type=F32)
        for i in range(4):
            t = 4 + i // 2
            full = tangent[:, i * 128 : (i + 1) * 128]
            half = tangent[(i % 2) * 72 : (i % 2) * 72 + 72, t * 128 : (t + 1) * 128]
            if d:
                tb[d - 1, i, 0:ROWS] = full.astype(BF16)
                tb[d - 1, i, ROWS:CHUNK] = half.astype(BF16)
            else:
                town[i, 0:ROWS] = full
                town[i, ROWS:CHUNK] = half
        if d:
            for o in OFFSETS + (0,):
                i = (a2 + o) % 4
                rs1[o, d] = send(
                    tb.at[d - 1, i], r1.at[d - 1, i], rs_send.at[o, d - 1], rs_recv.at[o, d - 1], plane(g, a2)
                )
    hid_t[...] = jnp.transpose(jnp.concatenate([hidden, jnp.zeros((112, 256), F32)], axis=0)).astype(BF16)

    def reduced(i):
        return ((town[i] + r1[0, i].astype(F32)) + r1[1, i].astype(F32)) + r1[2, i].astype(F32)

    rs2 = []
    for o in OFFSETS + (0,):
        for d in OFFSETS:
            rs1[o, d].wait_recv()
        i = (a2 + o) % 4
        if o:
            p2s[o - 1] = reduced(i).astype(BF16)
            rs2.append(send(p2s.at[o - 1], r2.at[o - 1], rs_send.at[4, o - 1], rs_recv.at[4, o - 1], plane(a1, i)))
    mine_sum = reduced(a2)
    for copy in rs2:
        copy.wait_recv()
    mine_sum = ((mine_sum + r2[0].astype(F32)) + r2[1].astype(F32)) + r2[2].astype(F32)

    zs[...] = mine_sum.astype(BF16)
    zp = send(zs, rz0, z_send.at[0], z_recv.at[0], (y, x, z - sg, c))
    zp.wait_recv()
    total = mine_sum + rz0[...].astype(F32)
    zes[...] = total.astype(BF16)
    zc = [
        send(zes, rz.at[k], z_send.at[1 + k], z_recv.at[1 + k], (y, x, (z + sg * (k + 1) + 8) % 8, c))
        for k in range(3)
    ]
    resp_f, resp_h = total[0:ROWS], total[ROWS:CHUNK]
    for k in range(3):
        zc[k].wait_recv()
        resp_f = resp_f + jnp.dot(amat[k], rz[k, 0:ROWS, :], preferred_element_type=F32)
        resp_h = resp_h + jnp.dot(amat_h[k], rz[k, ROWS:CHUNK, :], preferred_element_type=F32)
    base = c * HALF + a1 * GROUP
    sig_f = sigma[:, pl.ds(pl.multiple_of(base + a2 * 128, 128), 128)]
    sig_h = sigma[:, pl.ds(pl.multiple_of(base + (4 + a2 // 2) * 128, 128), 128)]
    c4[m, 0:ROWS] = (rho_s[...] * sig_f * (resp_f * SCALE)).astype(BF16)
    c4[m, ROWS:CHUNK] = (rho_s[half_rows, :] * sig_h * (resp_h * SCALE)).astype(BF16)

    cg1 = along(c4, cg_send, cg_recv)
    cg2 = [spread(c4, m, 0, cg_send, cg_recv)]
    for d, copy in zip(OFFSETS, cg1):
        copy.wait_recv()
        cg2.append(spread(c4, behind(d), d, cg_send, cg_recv))

    def assemble(ref, g):
        for i in range(4):
            cg[:, i * 128 : (i + 1) * 128] = ref[g * 4 + i, 0:ROWS, :]
        for i in range(2):
            both = [ref[g * 4 + 2 * i + u, ROWS:CHUNK, :].astype(F32) for u in range(2)]
            cg[:, (4 + i) * 128 : (5 + i) * 128] = jnp.concatenate(both, axis=0).astype(BF16)

    sums = (zero, zero, zero)
    cxs = []
    for n, d in enumerate((0,) + OFFSETS):
        if d:
            for copies in cg2:
                copies[n - 1].wait_recv()
        g = (a1 - d + 4) % 4
        block4 = pl.ds(pl.multiple_of(g * 4, 4), 4)
        cxs.append(send(c4.at[block4], cx.at[block4], cx_send.at[d], cx_recv.at[d], partner))
        assemble(c4, g)

        def image(k, sums):
            s0, s1, ss = sums
            part = pl.ds(pl.multiple_of(g * GROUP + k * 256, 256), 256)
            cols = cg[:, pl.ds(pl.multiple_of(k * 256, 256), 256)]
            fold = lambda a: jnp.sum(a.reshape(16, 8, 256), axis=0)
            for u in range(2):
                im = jnp.dot(hid_t[u * 128 : (u + 1) * 128, 0:ROWS], cols, preferred_element_type=F32) * SCALE
                if u == 0:
                    img[0, :, part] = im
                s0 = s0 + fold(im * v0[u, :, part].astype(F32))
                s1 = s1 + fold(im * v1[u, :, part].astype(F32))
                ss = ss + fold(im * im)
            return s0, s1, ss

        sums = lax.fori_loop(0, 3, image, sums)

    lines = [jnp.sum(s[:, 0:128] + s[:, 128:256], axis=0, keepdims=True) for s in sums + (s00, s01, s11)]
    lines.append(jnp.zeros((2, 128), F32))
    red_s[0] = jnp.concatenate(lines, axis=0)
    ras = []
    for k in range(1, 16):
        o = (p + k) % 16
        ras.append(send(red_s.at[0], red_a.at[k - 1], ra_send.at[k - 1], ra_recv.at[k - 1], (o // 4, o % 4, z, c)))

    for copy in cxs:
        copy.wait_recv()
    for g in range(4):
        assemble(cx, g)

        def image_other(k, carry):
            part = pl.ds(pl.multiple_of(g * GROUP + k * 256, 256), 256)
            cols = cg[:, pl.ds(pl.multiple_of(k * 256, 256), 256)]
            img[1, :, part] = jnp.dot(hid_t[0:128, 0:ROWS], cols, preferred_element_type=F32) * SCALE
            return carry

        lax.fori_loop(0, 3, image_other, 0)

    acc = red_s[0]
    for k in range(15):
        ras[k].wait_recv()
        acc = acc + red_a[k]
    red_s[1] = acc
    rbs = []
    for k in range(1, 16):
        o = (q + k) % 16
        rbs.append(send(red_s.at[1], red_b.at[k - 1], rb_send.at[k - 1], rb_recv.at[k - 1], (y, x, o // 2, o % 2)))
    for k in range(15):
        rbs[k].wait_recv()
        acc = acc + red_b[k]
    scal = jnp.sum(acc, axis=1, keepdims=True) * (1.0 / ENTRIES)
    c0, c1, norm, g00, g01, g11 = [scal[k : k + 1, 0:1] for k in range(6)]
    norm = norm - 2.0 * (c0 * c0 + c1 * c1) + (c0 * c0 * g00 + 2.0 * (c0 * c1) * g01 + c1 * c1 * g11)
    beta = jnp.sqrt(norm)
    hess[...] = jnp.concatenate([c0, c1, beta], axis=1)
    inv = 1.0 / beta
    for u, (w0, w1, start) in enumerate(((v0.at[0], v1.at[0], c * HALF), (v0x, v1x, (1 - c) * HALF))):

        def finish(k, carry):
            part = pl.ds(pl.multiple_of(k * 256, 256), 256)
            resid = (img[u, :, part] - c0 * w0[:, part].astype(F32)) - c1 * w1[:, part].astype(F32)
            out[:, pl.ds(pl.multiple_of(start + k * 256, 256), 256)] = (resid * inv).astype(BF16)
            return carry

        lax.fori_loop(0, HALF // 256, finish, 0)

    for copy in first + core + second + [pre_copy] + list(rs1.values()) + rs2 + [zp] + zc + cg1 + sum(cg2, []) + cxs + ras + rbs:
        copy.wait_send()


def body(tokens, w_gate, w_up, basis, routes, gates, rho, sigma):
    anywhere = pl.BlockSpec(memory_space=pl.ANY)
    vmem = pl.BlockSpec(memory_space=pltpu.VMEM)
    dma = pltpu.SemaphoreType.DMA
    scratch = [
        pltpu.VMEM((2, 256), jnp.int32),
        pltpu.VMEM((2, 256), F32),
        pltpu.VMEM((1, 16), F32),
        pltpu.VMEM((1, D), F32),
        pltpu.VMEM((256, 8), F32),
        pltpu.VMEM((16, HALF), BF16),
        pltpu.VMEM((2, HALF, 256), BF16),
        pltpu.VMEM((2, 128, HALF), BF16),
        pltpu.VMEM((2, 128, HALF), BF16),
        pltpu.VMEM((128, HALF), BF16),
        pltpu.VMEM((128, HALF), BF16),
        pltpu.VMEM((16, 8, MSG), BF16),
        pltpu.VMEM((ROWS, HALF), BF16),
        pltpu.VMEM((4, 128, 128), F32),
        pltpu.VMEM((8, 384), F32),
        pltpu.VMEM((ROWS, 128), F32),
        pltpu.VMEM((2, ROWS, 256), F32),
        pltpu.VMEM((2, ROWS, 256), F32),
        pltpu.VMEM((ROWS, 256), BF16),
        pltpu.VMEM((256, 256), BF16),
        pltpu.VMEM((3, 4, CHUNK, 128), BF16),
        pltpu.VMEM((3, 4, CHUNK, 128), BF16),
        pltpu.VMEM((4, CHUNK, 128), F32),
        pltpu.VMEM((3, CHUNK, 128), BF16),
        pltpu.VMEM((3, CHUNK, 128), BF16),
        pltpu.VMEM((CHUNK, 128), BF16),
        pltpu.VMEM((CHUNK, 128), BF16),
        pltpu.VMEM((CHUNK, 128), BF16),
        pltpu.VMEM((3, CHUNK, 128), BF16),
        pltpu.VMEM((3, ROWS, ROWS), BF16),
        pltpu.VMEM((3, 72, 72), BF16),
        pltpu.VMEM((256, 256), F32),
        pltpu.VMEM((ROWS, 128), F32),
        pltpu.VMEM((16, CHUNK, 128), BF16),
        pltpu.VMEM((16, CHUNK, 128), BF16),
        pltpu.VMEM((ROWS, GROUP), BF16),
        pltpu.VMEM((2, 128, HALF), F32),
        pltpu.VMEM((15, 8, 128), F32),
        pltpu.VMEM((15, 8, 128), F32),
        pltpu.VMEM((2, 8, 128), F32),
        dma((11,)),
        dma((5,)), dma((5,)),
        dma((5, 3)), dma((5, 3)),
        dma((5, 3)), dma((5, 3)),
        dma((4,)), dma((4,)),
        dma((5, 3)), dma((5, 3)),
        dma((4,)), dma((4,)),
        dma((15,)), dma((15,)),
        dma((15,)), dma((15,)),
    ]
    operands = (tokens, w_gate, w_up, basis, routes.T, gates.T, rho.reshape(1, 16), sigma.reshape(1, D))
    operands = [pltpu.with_memory_space_constraint(a, pltpu.HBM) for a in operands]
    out, hess = pl.pallas_call(
        kernel,
        out_shape=(jax.ShapeDtypeStruct((128, D), BF16), jax.ShapeDtypeStruct((1, 3), F32)),
        in_specs=[anywhere] * 8,
        out_specs=(vmem, vmem),
        scratch_shapes=scratch,
        compiler_params=pltpu.CompilerParams(
            collective_id=0, has_side_effects=True, vmem_limit_bytes=26 * 1024 * 1024
        ),
        name="arnoldi",
    )(*operands)
    return out, hess.T


def solution(mesh):
    finer = Mesh(mesh.devices.reshape(4, 4, 8, 2), AXES)
    in_specs = (
        P(DP, None),
        P(None, EXPERT_DP),
        P(None, EXPERT_DP),
        P(None, EXPERT_DP, None),
        P(),
        P(),
        P(DP),
        P(),
    )
    out_specs = (P(EXPERT_DP, None), P())
    return jax.shard_map(body, mesh=finer, in_specs=in_specs, out_specs=out_specs, check_vma=False)
```

profile of v0, /device:TPU:1, one launch (start us, length us, event | category | flops | bytes accessed | tf_op | source)
XLA Modules:
  0.0 73.1 jit_solution(17464805427757918706)
XLA Ops:
  0.6 70.8 %arnoldi.1 = (bf16[128,6144]{1,0:T(8,128)(2,1)S(1)}, f32[1,3]{1,0:T(1,128)S(1)}) custom-call(bf16[16,6144]{1,0:T(8,128)(2,1)} %tok_hbm.1, bf16[6144,128]{1,0:T(8,128)(2,1)} %wg_hbm.1, bf16[6144,128]{1,0:T(8,128)(2,1)} %wu_hbm.1, bf16[2,128,6144]{2,1,0:T(8,128)(2,1)} %basis_hbm.1, s32[2,256]{1,0:T(2,128)} %bitcast.7, f32[2,256]{1,0:T(2,128)} %bitcast.8, ...), custom_call_target="tpu_custom_call" | custom-call | tf_op jit(solution)/shard_map/arnoldi/pallas_call | solution.py:471
  71.5 1.1 %copy.12 = bf16[128,6144]{1,0:T(8,128)(2,1)} copy(bf16[128,6144]{1,0:T(8,128)(2,1)S(1)} %get-tuple-element.8) | data formatting | bytes 3145728
  72.6 0.5 copy.13
where the time goes:
time: 73.2 us; the launch traced here: 73.1 us
  Pallas kernels  70.8 us (97%)
  local copies, waits for them, and re-layouts  1.66 us (2%)
    pallas_call x1, Pallas kernels, body(): pl.pallas_call(kernel, out_shape=(jax.ShapeDtypeStruct((128, D), BF16), j...  70.8 us
    unnamed x2, local copies, waits for them, and re-layouts  1.66 us

commit v1 on v0

--- a/solution.py
+++ b/solution.py
@@ -55,9 +55,9 @@
     tok_hbm, wg_hbm, wu_hbm, basis_hbm, routes_hbm, gates_hbm, rho_hbm, sigma_hbm,
     out, hess,
     routes, gates, rho, sigma, cols, tokv, wbuf, v0, v1, v0x, v1x, gm, gd, exf, exs, side_main, pre_s, pre_r, hid, hid_t,
-    tb, r1, town, p2s, r2, zs, rz0, zes, rz, amat, amat_h, rank_s, rho_s, c4, cx, cg, img,
+    tb, r1, town, p2s, r2, tb0, r10, town0, p2s0, r20, held, sq_own, sq_out, sq_in, zs, rz0, zes, rz, amat, amat_h, rank_s, rho_s, c4, cx, cg, img,
     red_a, red_b, red_s,
-    loc_sem, core_send, core_recv, ag_send, ag_recv, rs_send, rs_recv, z_send, z_recv,
+    loc_sem, core_send, core_recv, ag_send, ag_recv, rs_send, rs_recv, rt_send, rt_recv, sq_send, sq_recv, z_send, z_recv,
     cg_send, cg_recv, cx_send, cx_recv, ra_send, ra_recv, rb_send, rb_recv,
 ):
     y, x, z, c = [lax.axis_index(name) for name in AXES]
@@ -258,54 +258,92 @@
     hidden = jnp.concatenate(hidden, axis=1)
     hid[...] = hidden.astype(BF16)
 
-    rs1 = {}
-    for d in OFFSETS + (0,):
-        g = (a1 + d) % 4
+    def tangents(vector, parts_out, own_out, g, d):
         part = pl.ds(pl.multiple_of(g * GROUP, GROUP), GROUP)
-        rows = v1[:, :, part].reshape(256, GROUP)
+        rows = vector[:, :, part].reshape(256, GROUP)
         tangent = jnp.dot(hid[...], rows, preferred_element_type=F32)
         for i in range(4):
             t = 4 + i // 2
             full = tangent[:, i * 128 : (i + 1) * 128]
             half = tangent[(i % 2) * 72 : (i % 2) * 72 + 72, t * 128 : (t + 1) * 128]
             if d:
-                tb[d - 1, i, 0:ROWS] = full.astype(BF16)
-                tb[d - 1, i, ROWS:CHUNK] = half.astype(BF16)
+                parts_out[d - 1, i, 0:ROWS] = full.astype(BF16)
+                parts_out[d - 1, i, ROWS:CHUNK] = half.astype(BF16)
             else:
-                town[i, 0:ROWS] = full
-                town[i, ROWS:CHUNK] = half
-        if d:
-            for o in OFFSETS + (0,):
-                i = (a2 + o) % 4
-                rs1[o, d] = send(
-                    tb.at[d - 1, i], r1.at[d - 1, i], rs_send.at[o, d - 1], rs_recv.at[o, d - 1], plane(g, a2)
+                own_out[i, 0:ROWS] = full
+                own_out[i, ROWS:CHUNK] = half
+
+    def reduce_first(parts_out, landing, d, s_sem, r_sem):
+        return {
+            (o, d): send(
+                parts_out.at[d - 1, (a2 + o) % 4], landing.at[d - 1, (a2 + o) % 4],
+                s_sem.at[o, d - 1], r_sem.at[o, d - 1], plane((a1 + d) % 4, a2),
+            )
+            for o in OFFSETS + (0,)
+        }
+
+    def reduce_second(copies, own_out, landing, parts_two, landing_two, s_sem, r_sem):
+        def reduced(i):
+            return ((own_out[i] + landing[0, i].astype(F32)) + landing[1, i].astype(F32)) + landing[2, i].astype(F32)
+
+        later = []
+        for o in OFFSETS + (0,):
+            for d in OFFSETS:
+                copies[o, d].wait_recv()
+            i = (a2 + o) % 4
+            if o:
+                parts_two[o - 1] = reduced(i).astype(BF16)
+                later.append(
+                    send(
+                        parts_two.at[o - 1], landing_two.at[o - 1],
+                        s_sem.at[4, o - 1], r_sem.at[4, o - 1], plane(a1, i),
+                    )
                 )
+        return later, reduced(a2)
+
+    rs1 = {}
+    for d in OFFSETS:
+        tangents(v1, tb, town, (a1 + d) % 4, d)
+        rs1.update(reduce_first(tb, r1, d, rs_send, rs_recv))
+    tangents(v1, tb, town, a1, 0)
+    square = lax.dot_general(hid[...], hid[...], (((1,), (1,)), ((), ())), preferred_element_type=F32)
+    corner = jnp.concatenate([square[128:ROWS, 128:ROWS], jnp.zeros((16, 112), F32)], axis=1)
+    sq_own[...] = jnp.concatenate([square[:, 0:128], corner], axis=0)
+    sq_out[0] = sq_own[...].astype(BF16)
     hid_t[...] = jnp.transpose(jnp.concatenate([hidden, jnp.zeros((112, 256), F32)], axis=0)).astype(BF16)
-
-    def reduced(i):
-        return ((town[i] + r1[0, i].astype(F32)) + r1[1, i].astype(F32)) + r1[2, i].astype(F32)
-
-    rs2 = []
-    for o in OFFSETS + (0,):
-        for d in OFFSETS:
-            rs1[o, d].wait_recv()
-        i = (a2 + o) % 4
-        if o:
-            p2s[o - 1] = reduced(i).astype(BF16)
-            rs2.append(send(p2s.at[o - 1], r2.at[o - 1], rs_send.at[4, o - 1], rs_recv.at[4, o - 1], plane(a1, i)))
-    mine_sum = reduced(a2)
+    for d in OFFSETS + (0,):
+        tangents(v0, tb0, town0, (a1 + d) % 4, d)
+
+    rs2, mine_sum = reduce_second(rs1, town, r1, p2s, r2, rs_send, rs_recv)
     for copy in rs2:
         copy.wait_recv()
     mine_sum = ((mine_sum + r2[0].astype(F32)) + r2[1].astype(F32)) + r2[2].astype(F32)
+    held[...] = mine_sum
 
     zs[...] = mine_sum.astype(BF16)
     zp = send(zs, rz0, z_send.at[0], z_recv.at[0], (y, x, z - sg, c))
+    rs3 = {}
+    for d in OFFSETS:
+        rs3.update(reduce_first(tb0, r10, d, rt_send, rt_recv))
+    squares = [
+        send(sq_out.at[0], sq_in.at[0, d - 1], sq_send.at[0, d - 1], sq_recv.at[0, d - 1], plane((a1 + d) % 4, a2))
+        for d in OFFSETS
+    ]
     zp.wait_recv()
     total = mine_sum + rz0[...].astype(F32)
     zes[...] = total.astype(BF16)
-    zc = [
-        send(zes, rz.at[k], z_send.at[1 + k], z_recv.at[1 + k], (y, x, (z + sg * (k + 1) + 8) % 8, c))
-        for k in range(3)
+    zc = {
+        k: send(zes, rz.at[k], z_send.at[1 + k], z_recv.at[1 + k], (y, x, (z + sg * (k + 1) + 8) % 8, c))
+        for k in (2, 1, 0)
+    }
+    rs4, mine_other = reduce_second(rs3, town0, r10, p2s0, r20, rt_send, rt_recv)
+    for copy in squares:
+        copy.wait_recv()
+    sq_sum = ((sq_own[...] + sq_in[0, 0].astype(F32)) + sq_in[0, 1].astype(F32)) + sq_in[0, 2].astype(F32)
+    sq_out[1] = sq_sum.astype(BF16)
+    squares_two = [
+        send(sq_out.at[1], sq_in.at[1, d - 1], sq_send.at[1, d - 1], sq_recv.at[1, d - 1], plane(a1, (a2 + d) % 4))
+        for d in OFFSETS
     ]
     resp_f, resp_h = total[0:ROWS], total[ROWS:CHUNK]
     for k in range(3):
@@ -331,8 +369,44 @@
             both = [ref[g * 4 + 2 * i + u, ROWS:CHUNK, :].astype(F32) for u in range(2)]
             cg[:, (4 + i) * 128 : (5 + i) * 128] = jnp.concatenate(both, axis=0).astype(BF16)
 
-    sums = (zero, zero, zero)
+    for copy in rs4 + squares_two:
+        copy.wait_recv()
+    mine_other = ((mine_other + r20[0].astype(F32)) + r20[1].astype(F32)) + r20[2].astype(F32)
+    sq_sum = ((sq_sum + sq_in[1, 0].astype(F32)) + sq_in[1, 1].astype(F32)) + sq_in[1, 2].astype(F32)
+    sq_b = sq_sum.astype(BF16)
+    cot = c4[m].astype(F32)
+    line = lambda a: jnp.sum(a, axis=0, keepdims=True)
+    both = [c4[a1 * 4 + (a2 // 2) * 2 + u, ROWS:CHUNK, :].astype(F32) for u in range(2)]
+    tiles = jnp.concatenate([cot[0:ROWS], jnp.concatenate(both, axis=0)], axis=1)
+    tiles_b = tiles.astype(BF16)
+    mixed = jnp.dot(sq_b[0:ROWS], tiles_b[0:128], preferred_element_type=F32)
+    mixed_low = jnp.dot(sq_b[ROWS:160, 0:16], tiles_b[128:ROWS], preferred_element_type=F32)
+    quad = line(tiles[0:128] * mixed[0:128]) + line(tiles[128:ROWS] * (2.0 * mixed[128:ROWS] + mixed_low))
+    lines = [
+        line(cot * mine_other) * SCALE,
+        line(cot * held[...]) * SCALE,
+        (quad[:, 0:128] + 0.5 * quad[:, 128:256]) * (SCALE * SCALE),
+    ] + [line(s[:, 0:128] + s[:, 128:256]) for s in (s00, s01, s11)]
+    lines.append(jnp.zeros((2, 128), F32))
+    red_s[0] = jnp.concatenate(lines, axis=0)
+    ras = []
+    for k in range(1, 16):
+        o = (p + k) % 16
+        ras.append(send(red_s.at[0], red_a.at[k - 1], ra_send.at[k - 1], ra_recv.at[k - 1], (o // 4, o % 4, z, c)))
+
+    def rows_image(ref, u, g):
+        assemble(ref, g)
+
+        def image(k, carry):
+            part = pl.ds(pl.multiple_of(g * GROUP + k * 256, 256), 256)
+            cols_k = cg[:, pl.ds(pl.multiple_of(k * 256, 256), 256)]
+            img[u, :, part] = jnp.dot(hid_t[0:128, 0:ROWS], cols_k, preferred_element_type=F32) * SCALE
+            return carry
+
+        lax.fori_loop(0, 3, image, 0)
+
     cxs = []
+    rbs = []
     for n, d in enumerate((0,) + OFFSETS):
         if d:
             for copies in cg2:
@@ -340,54 +414,23 @@
         g = (a1 - d + 4) % 4
         block4 = pl.ds(pl.multiple_of(g * 4, 4), 4)
         cxs.append(send(c4.at[block4], cx.at[block4], cx_send.at[d], cx_recv.at[d], partner))
-        assemble(c4, g)
-
-        def image(k, sums):
-            s0, s1, ss = sums
-            part = pl.ds(pl.multiple_of(g * GROUP + k * 256, 256), 256)
-            cols = cg[:, pl.ds(pl.multiple_of(k * 256, 256), 256)]
-            fold = lambda a: jnp.sum(a.reshape(16, 8, 256), axis=0)
-            for u in range(2):
-                im = jnp.dot(hid_t[u * 128 : (u + 1) * 128, 0:ROWS], cols, preferred_element_type=F32) * SCALE
-                if u == 0:
-                    img[0, :, part] = im
-                s0 = s0 + fold(im * v0[u, :, part].astype(F32))
-                s1 = s1 + fold(im * v1[u, :, part].astype(F32))
-                ss = ss + fold(im * im)
-            return s0, s1, ss
-
-        sums = lax.fori_loop(0, 3, image, sums)
-
-    lines = [jnp.sum(s[:, 0:128] + s[:, 128:256], axis=0, keepdims=True) for s in sums + (s00, s01, s11)]
-    lines.append(jnp.zeros((2, 128), F32))
-    red_s[0] = jnp.concatenate(lines, axis=0)
-    ras = []
-    for k in range(1, 16):
-        o = (p + k) % 16
-        ras.append(send(red_s.at[0], red_a.at[k - 1], ra_send.at[k - 1], ra_recv.at[k - 1], (o // 4, o % 4, z, c)))
+        if n == 3:
+            acc = red_s[0]
+            for k in range(15):
+                ras[k].wait_recv()
+                acc = acc + red_a[k]
+            red_s[1] = acc
+            for k in range(1, 16):
+                o = (q + k) % 16
+                rbs.append(
+                    send(red_s.at[1], red_b.at[k - 1], rb_send.at[k - 1], rb_recv.at[k - 1], (y, x, o // 2, o % 2))
+                )
+        rows_image(c4, 0, g)
 
     for copy in cxs:
         copy.wait_recv()
     for g in range(4):
-        assemble(cx, g)
-
-        def image_other(k, carry):
-            part = pl.ds(pl.multiple_of(g * GROUP + k * 256, 256), 256)
-            cols = cg[:, pl.ds(pl.multiple_of(k * 256, 256), 256)]
-            img[1, :, part] = jnp.dot(hid_t[0:128, 0:ROWS], cols, preferred_element_type=F32) * SCALE
-            return carry
-
-        lax.fori_loop(0, 3, image_other, 0)
-
-    acc = red_s[0]
-    for k in range(15):
-        ras[k].wait_recv()
-        acc = acc + red_a[k]
-    red_s[1] = acc
-    rbs = []
-    for k in range(1, 16):
-        o = (q + k) % 16
-        rbs.append(send(red_s.at[1], red_b.at[k - 1], rb_send.at[k - 1], rb_recv.at[k - 1], (y, x, o // 2, o % 2)))
+        rows_image(cx, 1, g)
     for k in range(15):
         rbs[k].wait_recv()
         acc = acc + red_b[k]
@@ -407,7 +450,7 @@
 
         lax.fori_loop(0, HALF // 256, finish, 0)
 
-    for copy in first + core + second + [pre_copy] + list(rs1.values()) + rs2 + [zp] + zc + cg1 + sum(cg2, []) + cxs + ras + rbs:
+    for copy in first + core + second + [pre_copy] + list(rs1.values()) + rs2 + [zp] + list(zc.values()) + list(rs3.values()) + rs4 + squares + squares_two + cg1 + sum(cg2, []) + cxs + ras + rbs:
         copy.wait_send()
 
 
@@ -441,6 +484,15 @@
         pltpu.VMEM((4, CHUNK, 128), F32),
         pltpu.VMEM((3, CHUNK, 128), BF16),
         pltpu.VMEM((3, CHUNK, 128), BF16),
+        pltpu.VMEM((3, 4, CHUNK, 128), BF16),
+        pltpu.VMEM((3, 4, CHUNK, 128), BF16),
+        pltpu.VMEM((4, CHUNK, 128), F32),
+        pltpu.VMEM((3, CHUNK, 128), BF16),
+        pltpu.VMEM((3, CHUNK, 128), BF16),
+        pltpu.VMEM((CHUNK, 128), F32),
+        pltpu.VMEM((160, 128), F32),
+        pltpu.VMEM((2, 160, 128), BF16),
+        pltpu.VMEM((2, 3, 160, 128), BF16),
         pltpu.VMEM((CHUNK, 128), BF16),
         pltpu.VMEM((CHUNK, 128), BF16),
         pltpu.VMEM((CHUNK, 128), BF16),
@@ -460,6 +512,8 @@
         dma((5,)), dma((5,)),
         dma((5, 3)), dma((5, 3)),
         dma((5, 3)), dma((5, 3)),
+        dma((5, 3)), dma((5, 3)),
+        dma((2, 3)), dma((2, 3)),
         dma((4,)), dma((4,)),
         dma((5, 3)), dma((5, 3)),
         dma((4,)), dma((4,)),
@@ -475,7 +529,7 @@
         out_specs=(vmem, vmem),
         scratch_shapes=scratch,
         compiler_params=pltpu.CompilerParams(
-            collective_id=0, has_side_effects=True, vmem_limit_bytes=26 * 1024 * 1024
+            collective_id=0, has_side_effects=True, vmem_limit_bytes=32 * 1024 * 1024
         ),
         name="arnoldi",
     )(*operands)

time: 73.2 us -> 70.4 us (0.962)
  Pallas kernels: 70.8 us -> 68 us
    pallas_call x1, Pallas kernels: 70.8 us -> 68 us  [body(): pl.pallas_call(kernel, out_shape=(jax.ShapeDtypeStruct((128, D), BF16), j...]
where the time goes in v1:
time: 70.4 us; the launch traced here: 70.3 us
  Pallas kernels  68 us (97%)
  local copies, waits for them, and re-layouts  1.66 us (2%)
    pallas_call x1, Pallas kernels, body(): pl.pallas_call(kernel, out_shape=(jax.ShapeDtypeStruct((128, D), BF16), j...  68 us
    unnamed x2, local copies, waits for them, and re-layouts  1.66 us

profile of v1, /device:TPU:1, one launch (start us, length us, event | category | flops | bytes accessed | tf_op | source)
XLA Modules:
  0.0 70.3 jit_solution(13914732144312508997)
XLA Ops:
  0.6 68.0 %arnoldi.1 = (bf16[128,6144]{1,0:T(8,128)(2,1)S(1)}, f32[1,3]{1,0:T(1,128)S(1)}) custom-call(bf16[16,6144]{1,0:T(8,128)(2,1)} %tok_hbm.1, bf16[6144,128]{1,0:T(8,128)(2,1)} %wg_hbm.1, bf16[6144,128]{1,0:T(8,128)(2,1)} %wu_hbm.1, bf16[2,128,6144]{2,1,0:T(8,128)(2,1)} %basis_hbm.1, s32[2,256]{1,0:T(2,128)} %bitcast.7, f32[2,256]{1,0:T(2,128)} %bitcast.8, ...), custom_call_target="tpu_custom_call" | custom-call | tf_op jit(solution)/shard_map/arnoldi/pallas_call | solution.py:525
  68.7 1.1 %copy.12 = bf16[128,6144]{1,0:T(8,128)(2,1)} copy(bf16[128,6144]{1,0:T(8,128)(2,1)S(1)} %get-tuple-element.8) | data formatting | bytes 3145728
  69.8 0.5 copy.13

commit v2 on v1

v2 whole, which is shorter than its diff:
```python
import functools
import math

import jax
import jax.numpy as jnp
from jax import lax
from jax.experimental import pallas as pl
from jax.experimental.pallas import tpu as pltpu
from jax.sharding import Mesh
from jax.sharding import PartitionSpec as P

D = 6144
FF = 8192
E = 4
HALF = 3072
GROUP = 768
SIDE = 128
MSG = HALF + SIDE + 512
ROWS = 144
CHUNK = 216
DP = ("dp_0", "dp_1")
EXPERT = ("expert_0", "expert_1")
EXPERT_DP = ("expert_0", "expert_1", "dp_0", "dp_1")
AXES = ("dp_0", "dp_1", "expert_0", "expert_1")
MESH = pl.DeviceIdType.MESH
F32 = jnp.float32
BF16 = jnp.bfloat16
SCALE = 1.0 / math.sqrt(FF)
KAPPA = E * FF / 256
ENTRIES = float(E * FF * D)
OFFSETS = (1, 3, 2)


def iota(shape, dim):
    return lax.broadcasted_iota(jnp.int32, shape, dim)


def parts(col):
    hi = col.astype(BF16)
    left = col - hi.astype(F32)
    mid = left.astype(BF16)
    low = (left - mid.astype(F32)).astype(BF16)
    return hi.astype(F32), mid.astype(F32), low.astype(F32)


def joined(side, first):
    return (side[:, first : first + 1] + side[:, first + 1 : first + 2]) + side[:, first + 2 : first + 3]


def slot_order(m):
    return jnp.concatenate([m[0:64], m[128:136], m[64:128], m[136:144]], axis=0)


def kernel(
    tok_hbm, wg_hbm, wu_hbm, basis_hbm, routes_hbm, gates_hbm, rho_hbm, sigma_hbm,
    out, hess,
    routes, gates, rho, sigma, cols, tokv, wbuf, v0, v1, v0x, v1x, gm, gd, exf, exs, side_main, pre_s, pre_r, hid, hid_t,
    tb, r1, town, p2s, r2, tb0, r10, town0, held, sq_own, sq_out, sq_in, zs, rz0, zes, rz, amat, amat_h, rank_s, rho_s, c4, cx, cg, img,
    red_a, red_b, red_s,
    loc_sem, core_send, core_recv, ag_send, ag_recv, rs_send, rs_recv, rt_send, rt_recv, sq_send, sq_recv, z_send, z_recv,
    cg_send, cg_recv, cx_send, cx_recv, ra_send, ra_recv, rb_send, rb_recv,
):
    y, x, z, c = [lax.axis_index(name) for name in AXES]
    a1 = y * (1 - c) + x * c
    a2 = x * (1 - c) + y * c
    p = y * 4 + x
    q = z * 2 + c
    e = z // 2
    sg = 2 * (z % 2) - 1
    h = a2 % 2
    half_rows = pl.ds(pl.multiple_of(h * 72, 8), 72)

    def plane(b1, b2):
        return (b1 * (1 - c) + b2 * c, b2 * (1 - c) + b1 * c, z, c)

    def send(src, dst, s_sem, r_sem, device):
        copy = pltpu.make_async_remote_copy(
            src_ref=src, dst_ref=dst, send_sem=s_sem, recv_sem=r_sem, device_id=device, device_id_type=MESH
        )
        copy.start()
        return copy

    def local(src, dst, sem):
        copy = pltpu.make_async_copy(src, dst, sem)
        copy.start()
        return copy

    barrier = pltpu.get_barrier_semaphore()
    for k in range(1, 16):
        o = (p + k) % 16
        pl.semaphore_signal(barrier, inc=1, device_id=(o // 4, o % 4, z, c), device_id_type=MESH)
        o = (q + k) % 16
        pl.semaphore_signal(barrier, inc=1, device_id=(y, x, o // 2, o % 2), device_id_type=MESH)

    mine = pl.ds(pl.multiple_of(c * HALF, HALF), HALF)
    other = pl.ds(pl.multiple_of((1 - c) * HALF, HALF), HALF)
    small = [
        local(routes_hbm, routes, loc_sem.at[7]),
        local(gates_hbm, gates, loc_sem.at[8]),
        local(rho_hbm, rho, loc_sem.at[9]),
    ]
    loads = [
        local(tok_hbm.at[:, mine], tokv, loc_sem.at[0]),
        local(wg_hbm.at[mine, :], wbuf.at[0, :, pl.ds(0, 128)], loc_sem.at[1]),
        local(wu_hbm.at[mine, :], wbuf.at[0, :, pl.ds(128, 128)], loc_sem.at[2]),
        local(basis_hbm.at[1, :, mine], v1.at[0], loc_sem.at[3]),
        local(basis_hbm.at[0, :, mine], v0.at[0], loc_sem.at[4]),
        local(basis_hbm.at[1, :, other], v1x, loc_sem.at[5]),
        local(basis_hbm.at[0, :, other], v0x, loc_sem.at[6]),
        local(sigma_hbm, sigma, loc_sem.at[10]),
    ]
    for copy in small:
        copy.wait()

    cols[...] = jnp.transpose(
        jnp.concatenate([routes[...].astype(F32), gates[...], jnp.zeros((4, 256), F32)], axis=0)
    )
    own = cols[pl.ds(pl.multiple_of(p * 16, 16), 16), :]
    ef = e.astype(F32)
    hit0 = own[:, 0:1] == ef
    hit1 = own[:, 1:2] == ef
    member = hit0.astype(F32) + hit1.astype(F32)
    gate_tok = jnp.where(hit0, own[:, 2:3], 0.0) + jnp.where(hit1, own[:, 3:4], 0.0)
    tri = (iota((16, 16), 1) <= iota((16, 16), 0)).astype(F32).astype(BF16)
    member_b = jnp.broadcast_to(member, (16, 128))
    rank = jnp.dot(tri, member_b.astype(BF16), preferred_element_type=F32)
    lane = iota((16, 128), 1)
    place_t = jnp.where((rank - 1.0 == lane.astype(F32)) & (member_b > 0), 1.0, 0.0)
    place = jnp.transpose(place_t)[0:16, :].astype(BF16)
    diagonal = iota((16, 16), 0) == iota((16, 16), 1)
    rho_tok = jnp.sum(jnp.where(diagonal, jnp.broadcast_to(rho[...], (16, 16)), 0.0), axis=1, keepdims=True)
    r_hi, r_mid, r_low = parts(rho_tok)
    g_hi, g_mid, g_low = parts(gate_tok)
    side_in = jnp.zeros((16, 128), F32)
    for index, col in enumerate((r_hi, r_mid, r_low, g_hi, g_mid, g_low)):
        side_in = jnp.where(lane == index, col, side_in)
    side = jnp.dot(place, side_in.astype(BF16), preferred_element_type=F32)
    m = a1 * 4 + a2
    gm[m, :, HALF : HALF + SIDE] = side[0:8].astype(BF16)
    gm[m, :, HALF + SIDE + 384 : MSG] = jnp.broadcast_to(side[8:9], (8, 128)).astype(BF16)
    loads[0].wait()
    picked = jnp.dot(place, tokv[...], preferred_element_type=F32)
    gm[m, :, 0:HALF] = picked[0:8].astype(BF16)
    for r in range(8):
        exs[r : r + 1, :] = picked[8:9, r * 384 : (r + 1) * 384]
    gm[m, :, HALF + SIDE : HALF + SIDE + 384] = exs[...].astype(BF16)

    pl.semaphore_wait(barrier, 30)

    def spread(ref, lap, s_sem, r_sem):
        index = a1 * 4 + (a2 + 4 - lap) % 4
        return {
            (lap, d): send(
                ref.at[index], ref.at[index], s_sem.at[lap, d - 1], r_sem.at[lap, d - 1], plane((a1 + d) % 4, a2)
            )
            for d in OFFSETS
        }

    def pass_on(copies, ref, lap, s_sem, r_sem):
        d = 1 if lap in (0, 3) else 3
        copies[lap, d].wait_recv()
        index = ((a1 + 4 - d) % 4) * 4 + (a2 + 4 - lap) % 4
        copies[lap, 2] = send(
            ref.at[index], ref.at[index], s_sem.at[lap, 1], r_sem.at[lap, 1], plane((a1 + d) % 4, a2)
        )

    def along(ref, s_sem, r_sem):
        return [
            send(ref.at[m], ref.at[m], s_sem.at[4, d - 1], r_sem.at[4, d - 1], plane(a1, (a2 + d) % 4))
            for d in OFFSETS
        ]

    def relay(first, copies, ref, s_sem, r_sem):
        for d, copy in zip(OFFSETS, first):
            copy.wait_recv()
            copies.update(spread(ref, d, s_sem, r_sem))

    def finish_laps(copies, ref, s_sem, r_sem):
        for lap in OFFSETS:
            pass_on(copies, ref, lap, s_sem, r_sem)

    def landed(copies, d):
        for lap in range(4):
            copies[lap, d].wait_recv()

    first = along(gm, ag_send, ag_recv)
    second = spread(gm, 0, ag_send, ag_recv)
    partner = (y, x, z, 1 - c)
    core = [
        send(wg_hbm.at[other, :], wbuf.at[1, :, pl.ds(0, 128)], core_send.at[0], core_recv.at[0], partner),
        send(wu_hbm.at[other, :], wbuf.at[1, :, pl.ds(128, 128)], core_send.at[1], core_recv.at[1], partner),
        send(basis_hbm.at[1, :, other], v1.at[1], core_send.at[2], core_recv.at[2], partner),
        send(basis_hbm.at[0, :, other], v0.at[1], core_send.at[3], core_recv.at[3], partner),
    ]

    relay(first, second, gm, ag_send, ag_recv)

    for d in OFFSETS:
        landed(second, d)
    for copy in loads[1:]:
        copy.wait()
    for copy in core:
        copy.wait_recv()

    def source(o):
        return o * (1 - c) + ((o % 4) * 4 + o // 4) * c

    for k in range(8):
        pair = [gm[source(2 * k + u), :, 0:HALF].astype(F32) for u in range(2)]
        gd[16 * k : 16 * k + 16, :] = jnp.concatenate(pair, axis=0).astype(BF16)
    for o in range(16):
        block_o = gm[source(o)][:, HALF:MSG].astype(F32)
        side_main[8 * o : 8 * o + 8, :] = block_o[:, 0:SIDE]
        for t in range(4):
            exf[t, 8 * o : 8 * o + 8, :] = block_o[:, SIDE + t * 128 : SIDE + (t + 1) * 128]
    for r in range(8):
        for t in range(3):
            f = r * 384 + t * 128
            gd[128:144, f : f + 128] = exf[t, pl.ds(r, 16, stride=8), :].astype(BF16)
    side_main[128:144, :] = exf[3, pl.ds(0, 16, stride=8), :]

    for u in range(2):
        pre_s[u] = jnp.dot(gd[...], wbuf[u], preferred_element_type=F32)
    pre_copy = send(pre_s, pre_r, core_send.at[4], core_recv.at[4], partner)
    side_all = side_main[...]
    rho_slot = slot_order(jnp.broadcast_to(joined(side_all, 0), (ROWS, 128)))
    rho_s[...] = KAPPA * rho_slot
    gate_slot = slot_order(jnp.broadcast_to(joined(side_all, 3), (ROWS, 128)))
    pre_copy.wait_recv()
    hidden = []
    for u in range(2):
        both = slot_order(pre_s[u] + pre_r[1 - u])
        gate, up = both[:, 0:128], both[:, 128:256]
        hidden.append(gate / (1.0 + jnp.exp(-gate)) * up * gate_slot)
    hidden = jnp.concatenate(hidden, axis=1)
    hid[...] = hidden.astype(BF16)

    def tangents(vector, parts_out, own_out, g, d):
        part = pl.ds(pl.multiple_of(g * GROUP, GROUP), GROUP)
        rows = vector[:, :, part].reshape(256, GROUP)
        tangent = jnp.dot(hid[...], rows, preferred_element_type=F32)
        for i in range(4):
            t = 4 + i // 2
            full = tangent[:, i * 128 : (i + 1) * 128]
            half = tangent[(i % 2) * 72 : (i % 2) * 72 + 72, t * 128 : (t + 1) * 128]
            if d:
                parts_out[d - 1, i, 0:ROWS] = full.astype(BF16)
                parts_out[d - 1, i, ROWS:CHUNK] = half.astype(BF16)
            else:
                own_out[i, 0:ROWS] = full
                own_out[i, ROWS:CHUNK] = half

    def reduce_first(parts_out, landing, d, s_sem, r_sem):
        return {
            (o, d): send(
                parts_out.at[d - 1, (a2 + o) % 4], landing.at[d - 1, (a2 + o) % 4],
                s_sem.at[o, d - 1], r_sem.at[o, d - 1], plane((a1 + d) % 4, a2),
            )
            for o in OFFSETS + (0,)
        }

    def reduce_second(copies, own_out, landing, parts_two, landing_two, s_sem, r_sem):
        def reduced(i):
            return ((own_out[i] + landing[0, i].astype(F32)) + landing[1, i].astype(F32)) + landing[2, i].astype(F32)

        later = []
        for o in OFFSETS + (0,):
            for d in OFFSETS:
                copies[o, d].wait_recv()
            i = (a2 + o) % 4
            if o:
                parts_two[o - 1] = reduced(i).astype(BF16)
                later.append(
                    send(
                        parts_two.at[o - 1], landing_two.at[o - 1],
                        s_sem.at[4, o - 1], r_sem.at[4, o - 1], plane(a1, i),
                    )
                )
        return later, reduced(a2)

    rs1 = {}
    for d in OFFSETS:
        tangents(v1, tb, town, (a1 + d) % 4, d)
        rs1.update(reduce_first(tb, r1, d, rs_send, rs_recv))
    tangents(v1, tb, town, a1, 0)
    square = lax.dot_general(hid[...], hid[...], (((1,), (1,)), ((), ())), preferred_element_type=F32)
    corner = jnp.concatenate([square[128:ROWS, 128:ROWS], jnp.zeros((16, 112), F32)], axis=1)
    sq_own[...] = jnp.concatenate([square[:, 0:128], corner], axis=0)
    sq_out[...] = sq_own[...].astype(BF16)
    hid_t[...] = jnp.transpose(jnp.concatenate([hidden, jnp.zeros((112, 256), F32)], axis=0)).astype(BF16)
    for d in (1, 3):
        tangents(v0, tb0, town0, (a1 + d) % 4, d)

    rs2, mine_sum = reduce_second(rs1, town, r1, p2s, r2, rs_send, rs_recv)
    for copy in rs2:
        copy.wait_recv()
    mine_sum = ((mine_sum + r2[0].astype(F32)) + r2[1].astype(F32)) + r2[2].astype(F32)
    held[...] = mine_sum

    zs[...] = mine_sum.astype(BF16)
    zp = send(zs, rz0, z_send.at[0], z_recv.at[0], (y, x, z - sg, c))
    rs3 = {}
    for d in OFFSETS:
        if d == 2:
            tangents(v0, tb0, town0, (a1 + d) % 4, d)
        rs3.update(reduce_first(tb0, r10, d, rt_send, rt_recv))
    squares = [
        send(sq_out, sq_in.at[d - 1], sq_send.at[d - 1], sq_recv.at[d - 1], plane((a1 + d) % 4, a2))
        for d in OFFSETS
    ]
    zp.wait_recv()
    total = mine_sum + rz0[...].astype(F32)
    zes[...] = total.astype(BF16)
    zc = {
        k: send(zes, rz.at[k], z_send.at[1 + k], z_recv.at[1 + k], (y, x, (z + sg * (k + 1) + 8) % 8, c))
        for k in (2, 1, 0)
    }

    t_lane = iota((256, 128), 1)
    shift = jnp.where(t_lane == 1, sg, 0) + jnp.where(t_lane == 2, -sg, 0) + jnp.where(t_lane == 3, 2, 0)
    names = jnp.where(t_lane < 4, (e + shift + 4) & 3, -1)
    names = names.astype(F32)
    member4 = (cols[:, 0:1] == names).astype(F32) + (cols[:, 1:2] == names).astype(F32)
    low = iota((256, 256), 0)
    col = iota((256, 256), 1)
    tri_b = ((col <= low) & ((col >> 4) == (low >> 4))).astype(F32).astype(BF16)
    rank4 = jnp.dot(tri_b, member4.astype(BF16), preferred_element_type=F32)
    token = iota((256, 128), 0)
    block = token >> 4
    slot = rank4.astype(jnp.int32) - 1
    where_to = (block >> 3) * 72 + jnp.where(slot < 8, (block & 7) * 8 + slot, 64 + (block & 7))
    where_to = jnp.where(member4 > 0, where_to, -1000)
    onehot = (where_to[:, 0:1] == col).astype(F32)
    rank_s[...] = jnp.transpose(onehot)
    own_full = rank_s[0:ROWS, :].astype(BF16)
    own_half = rank_s[half_rows, :].astype(BF16)
    for k in range(3):
        theirs = (where_to[:, k + 1 : k + 2] == col).astype(F32).astype(BF16)
        amat[k] = jnp.dot(own_full, theirs, preferred_element_type=F32)[:, 0:ROWS].astype(BF16)
        theirs = (where_to[:, k + 1 : k + 2] - h * 72 == col).astype(F32).astype(BF16)
        amat_h[k] = jnp.dot(own_half, theirs, preferred_element_type=F32)[:, 0:72].astype(BF16)

    tangents(v0, tb0, town0, a1, 0)
    def gram(k, sums):
        s00, s01, s11 = sums
        part = pl.ds(pl.multiple_of(k * 256, 256), 256)
        for u in range(2):
            b0 = v0[u, :, part].astype(F32)
            b1 = v1[u, :, part].astype(F32)
            fold = lambda a: jnp.sum(a.reshape(16, 8, 256), axis=0)
            s00 = s00 + fold(b0 * b0)
            s01 = s01 + fold(b0 * b1)
            s11 = s11 + fold(b1 * b1)
        return s00, s01, s11

    zero = jnp.zeros((8, 256), F32)
    s00, s01, s11 = lax.fori_loop(0, HALF // 256, gram, (zero, zero, zero))

    resp_f, resp_h = total[0:ROWS], total[ROWS:CHUNK]
    for k in range(3):
        zc[k].wait_recv()
        resp_f = resp_f + jnp.dot(amat[k], rz[k, 0:ROWS, :], preferred_element_type=F32)
        resp_h = resp_h + jnp.dot(amat_h[k], rz[k, ROWS:CHUNK, :], preferred_element_type=F32)
    base = c * HALF + a1 * GROUP
    sig_f = sigma[:, pl.ds(pl.multiple_of(base + a2 * 128, 128), 128)]
    sig_h = sigma[:, pl.ds(pl.multiple_of(base + (4 + a2 // 2) * 128, 128), 128)]
    c4[m, 0:ROWS] = (rho_s[...] * sig_f * (resp_f * SCALE)).astype(BF16)
    c4[m, ROWS:CHUNK] = (rho_s[half_rows, :] * sig_h * (resp_h * SCALE)).astype(BF16)

    cg1 = along(c4, cg_send, cg_recv)
    cg2 = spread(c4, 0, cg_send, cg_recv)
    relay(cg1, cg2, c4, cg_send, cg_recv)

    def assemble(ref, g):
        for i in range(4):
            cg[:, i * 128 : (i + 1) * 128] = ref[g * 4 + i, 0:ROWS, :]
        for i in range(2):
            both = [ref[g * 4 + 2 * i + u, ROWS:CHUNK, :].astype(F32) for u in range(2)]
            cg[:, (4 + i) * 128 : (5 + i) * 128] = jnp.concatenate(both, axis=0).astype(BF16)

    for copy in list(rs3.values()) + squares:
        copy.wait_recv()
    line = lambda a: jnp.sum(a, axis=0, keepdims=True)
    dot0 = jnp.zeros((1, 128), F32)
    for i in range(4):
        partial = ((town0[i] + r10[0, i].astype(F32)) + r10[1, i].astype(F32)) + r10[2, i].astype(F32)
        dot0 = dot0 + line(c4[a1 * 4 + i].astype(F32) * partial)
    square = ((sq_own[...] + sq_in[0].astype(F32)) + sq_in[1].astype(F32)) + sq_in[2].astype(F32)
    sq_b = square.astype(BF16)
    assemble(c4, a1)
    mixed = jnp.dot(sq_b[0:ROWS], cg[0:128, :], preferred_element_type=F32)
    mixed_low = jnp.dot(sq_b[ROWS:160, 0:16], cg[128:ROWS, :], preferred_element_type=F32)
    quad = line(cg[0:128, :].astype(F32) * mixed[0:128])
    quad = quad + line(cg[128:ROWS, :].astype(F32) * (2.0 * mixed[128:ROWS] + mixed_low))
    quad = sum(quad[:, i * 128 : (i + 1) * 128] for i in range(6))
    lines = [
        dot0 * SCALE,
        line(c4[m].astype(F32) * held[...]) * SCALE,
        quad * (SCALE * SCALE),
    ] + [line(s[:, 0:128] + s[:, 128:256]) for s in (s00, s01, s11)]
    lines.append(jnp.zeros((2, 128), F32))
    red_s[0] = jnp.concatenate(lines, axis=0)
    ras = []
    for k in range(1, 16):
        o = (q + k) % 16
        ras.append(send(red_s.at[0], red_a.at[k - 1], ra_send.at[k - 1], ra_recv.at[k - 1], (y, x, o // 2, o % 2)))

    def rows_image(ref, u, g):
        assemble(ref, g)

        part = pl.ds(pl.multiple_of(g * GROUP, GROUP), GROUP)
        img[u, :, part] = jnp.dot(hid_t[0:128, 0:ROWS], cg[...], preferred_element_type=F32) * SCALE

    cxs = []
    rbs = []
    for n, d in enumerate((0,) + OFFSETS):
        if d:
            landed(cg2, d)
        g = (a1 - d + 4) % 4
        block4 = pl.ds(pl.multiple_of(g * 4, 4), 4)
        cxs.append(send(c4.at[block4], cx.at[block4], cx_send.at[d], cx_recv.at[d], partner))
        if n == 3:
            acc = red_s[0]
            for k in range(15):
                ras[k].wait_recv()
                acc = acc + red_a[k]
            red_s[1] = acc
            for k in range(1, 16):
                o = (p + k) % 16
                rbs.append(
                    send(red_s.at[1], red_b.at[k - 1], rb_send.at[k - 1], rb_recv.at[k - 1], (o // 4, o % 4, z, c))
                )
        rows_image(c4, 0, g)
        if n:
            cxs[n - 1].wait_recv()
            rows_image(cx, 1, (a2 - ((0,) + OFFSETS)[n - 1] + 4) % 4)

    cxs[3].wait_recv()
    rows_image(cx, 1, (a2 - 2 + 4) % 4)
    for k in range(15):
        rbs[k].wait_recv()
        acc = acc + red_b[k]
    scal = jnp.sum(acc, axis=1, keepdims=True) * (1.0 / ENTRIES)
    c0, c1, norm, g00, g01, g11 = [scal[k : k + 1, 0:1] for k in range(6)]
    norm = norm - 2.0 * (c0 * c0 + c1 * c1) + (c0 * c0 * g00 + 2.0 * (c0 * c1) * g01 + c1 * c1 * g11)
    beta = jnp.sqrt(norm)
    hess[...] = jnp.concatenate([c0, c1, beta], axis=1)
    inv = 1.0 / beta
    for u, (w0, w1, start) in enumerate(((v0.at[0], v1.at[0], c * HALF), (v0x, v1x, (1 - c) * HALF))):

        def finish(k, carry):
            part = pl.ds(pl.multiple_of(k * 256, 256), 256)
            resid = (img[u, :, part] - c0 * w0[:, part].astype(F32)) - c1 * w1[:, part].astype(F32)
            out[:, pl.ds(pl.multiple_of(start + k * 256, 256), 256)] = (resid * inv).astype(BF16)
            return carry

        lax.fori_loop(0, HALF // 256, finish, 0)

    for copy in first + core + list(second.values()) + [pre_copy] + list(rs1.values()) + rs2 + [zp] + list(zc.values()) + list(rs3.values()) + squares + cg1 + list(cg2.values()) + cxs + ras + rbs:
        copy.wait_send()


def body(tokens, w_gate, w_up, basis, routes, gates, rho, sigma):
    anywhere = pl.BlockSpec(memory_space=pl.ANY)
    vmem = pl.BlockSpec(memory_space=pltpu.VMEM)
    dma = pltpu.SemaphoreType.DMA
    scratch = [
        pltpu.VMEM((2, 256), jnp.int32),
        pltpu.VMEM((2, 256), F32),
        pltpu.VMEM((1, 16), F32),
        pltpu.VMEM((1, D), F32),
        pltpu.VMEM((256, 8), F32),
        pltpu.VMEM((16, HALF), BF16),
        pltpu.VMEM((2, HALF, 256), BF16),
        pltpu.VMEM((2, 128, HALF), BF16),
        pltpu.VMEM((2, 128, HALF), BF16),
        pltpu.VMEM((128, HALF), BF16),
        pltpu.VMEM((128, HALF), BF16),
        pltpu.VMEM((16, 8, MSG), BF16),
        pltpu.VMEM((ROWS, HALF), BF16),
        pltpu.VMEM((4, 128, 128), F32),
        pltpu.VMEM((8, 384), F32),
        pltpu.VMEM((ROWS, 128), F32),
        pltpu.VMEM((2, ROWS, 256), F32),
        pltpu.VMEM((2, ROWS, 256), F32),
        pltpu.VMEM((ROWS, 256), BF16),
        pltpu.VMEM((256, 256), BF16),
        pltpu.VMEM((3, 4, CHUNK, 128), BF16),
        pltpu.VMEM((3, 4, CHUNK, 128), BF16),
        pltpu.VMEM((4, CHUNK, 128), F32),
        pltpu.VMEM((3, CHUNK, 128), BF16),
        pltpu.VMEM((3, CHUNK, 128), BF16),
        pltpu.VMEM((3, 4, CHUNK, 128), BF16),
        pltpu.VMEM((3, 4, CHUNK, 128), BF16),
        pltpu.VMEM((4, CHUNK, 128), F32),
        pltpu.VMEM((CHUNK, 128), F32),
        pltpu.VMEM((160, 128), F32),
        pltpu.VMEM((160, 128), BF16),
        pltpu.VMEM((3, 160, 128), BF16),
        pltpu.VMEM((CHUNK, 128), BF16),
        pltpu.VMEM((CHUNK, 128), BF16),
        pltpu.VMEM((CHUNK, 128), BF16),
        pltpu.VMEM((3, CHUNK, 128), BF16),
        pltpu.VMEM((3, ROWS, ROWS), BF16),
        pltpu.VMEM((3, 72, 72), BF16),
        pltpu.VMEM((256, 256), F32),
        pltpu.VMEM((ROWS, 128), F32),
        pltpu.VMEM((16, CHUNK, 128), BF16),
        pltpu.VMEM((16, CHUNK, 128), BF16),
        pltpu.VMEM((ROWS, GROUP), BF16),
        pltpu.VMEM((2, 128, HALF), F32),
        pltpu.VMEM((15, 8, 128), F32),
        pltpu.VMEM((15, 8, 128), F32),
        pltpu.VMEM((2, 8, 128), F32),
        dma((11,)),
        dma((5,)), dma((5,)),
        dma((5, 3)), dma((5, 3)),
        dma((5, 3)), dma((5, 3)),
        dma((4, 3)), dma((4, 3)),
        dma((3,)), dma((3,)),
        dma((4,)), dma((4,)),
        dma((5, 3)), dma((5, 3)),
        dma((4,)), dma((4,)),
        dma((15,)), dma((15,)),
        dma((15,)), dma((15,)),
    ]
    operands = (tokens, w_gate, w_up, basis, routes.T, gates.T, rho.reshape(1, 16), sigma.reshape(1, D))
    operands = [pltpu.with_memory_space_constraint(a, pltpu.HBM) for a in operands]
    out, hess = pl.pallas_call(
        kernel,
        out_shape=(jax.ShapeDtypeStruct((128, D), BF16), jax.ShapeDtypeStruct((1, 3), F32)),
        in_specs=[anywhere] * 8,
        out_specs=(vmem, vmem),
        scratch_shapes=scratch,
        compiler_params=pltpu.CompilerParams(
            collective_id=0, has_side_effects=True, vmem_limit_bytes=32 * 1024 * 1024
        ),
        name="arnoldi",
    )(*operands)
    return out, hess.T


def solution(mesh):
    finer = Mesh(mesh.devices.reshape(4, 4, 8, 2), AXES)
    in_specs = (
        P(DP, None),
        P(None, EXPERT_DP),
        P(None, EXPERT_DP),
        P(None, EXPERT_DP, None),
        P(),
        P(),
        P(DP),
        P(),
    )
    out_specs = (P(EXPERT_DP, None), P())
    return jax.shard_map(body, mesh=finer, in_specs=in_specs, out_specs=out_specs, check_vma=False)
```

time: 70.4 us -> 65.8 us (0.935)
  Pallas kernels: 68 us -> 63.4 us
    pallas_call x1, Pallas kernels: 68 us -> 63.4 us  [body(): pl.pallas_call(kernel, out_shape=(jax.ShapeDtypeStruct((128, D), BF16), j...]
where the time goes in v2:
time: 65.8 us; the launch traced here: 65.7 us
  Pallas kernels  63.4 us (96%)
  local copies, waits for them, and re-layouts  1.66 us (3%)
    pallas_call x1, Pallas kernels, body(): pl.pallas_call(kernel, out_shape=(jax.ShapeDtypeStruct((128, D), BF16), j...  63.4 us
    unnamed x2, local copies, waits for them, and re-layouts  1.66 us

profile of v2, /device:TPU:1, one launch (start us, length us, event | category | flops | bytes accessed | tf_op | source)
XLA Modules:
  0.0 65.7 jit_solution(8071499760266716365)
XLA Ops:
  0.6 63.4 %arnoldi.1 = (bf16[128,6144]{1,0:T(8,128)(2,1)S(1)}, f32[1,3]{1,0:T(1,128)S(1)}) custom-call(bf16[16,6144]{1,0:T(8,128)(2,1)} %tok_hbm.1, bf16[6144,128]{1,0:T(8,128)(2,1)} %wg_hbm.1, bf16[6144,128]{1,0:T(8,128)(2,1)} %wu_hbm.1, bf16[2,128,6144]{2,1,0:T(8,128)(2,1)} %basis_hbm.1, s32[2,256]{1,0:T(2,128)} %bitcast.7, f32[2,256]{1,0:T(2,128)} %bitcast.8, ...), custom_call_target="tpu_custom_call" | custom-call | tf_op jit(solution)/shard_map/arnoldi/pallas_call | solution.py:529
  64.0 1.1 %copy.12 = bf16[128,6144]{1,0:T(8,128)(2,1)} copy(bf16[128,6144]{1,0:T(8,128)(2,1)S(1)} %get-tuple-element.8) | data formatting | bytes 3145728
  65.2 0.5 copy.13

commit v3 on v2

--- a/solution.py
+++ b/solution.py
@@ -86,11 +86,11 @@
         return copy
 
     barrier = pltpu.get_barrier_semaphore()
-    for k in range(1, 16):
-        o = (p + k) % 16
-        pl.semaphore_signal(barrier, inc=1, device_id=(o // 4, o % 4, z, c), device_id_type=MESH)
-        o = (q + k) % 16
-        pl.semaphore_signal(barrier, inc=1, device_id=(y, x, o // 2, o % 2), device_id_type=MESH)
+    greeted = [(y, x, z, 1 - c)]
+    greeted += [((y + d) % 4, x, z, c) for d in OFFSETS] + [(y, (x + d) % 4, z, c) for d in OFFSETS]
+    greeted += [(y, x, (z + sg * d + 8) % 8, c) for d in (-1, 1, -2, 3)]
+    for device in greeted:
+        pl.semaphore_signal(barrier, inc=1, device_id=device, device_id_type=MESH)
 
     mine = pl.ds(pl.multiple_of(c * HALF, HALF), HALF)
     other = pl.ds(pl.multiple_of((1 - c) * HALF, HALF), HALF)
@@ -145,7 +145,7 @@
         exs[r : r + 1, :] = picked[8:9, r * 384 : (r + 1) * 384]
     gm[m, :, HALF + SIDE : HALF + SIDE + 384] = exs[...].astype(BF16)
 
-    pl.semaphore_wait(barrier, 30)
+    pl.semaphore_wait(barrier, 11)
 
     def spread(ref, lap, s_sem, r_sem):
         index = a1 * 4 + (a2 + 4 - lap) % 4
@@ -414,11 +414,6 @@
     cxs = []
     rbs = []
     for n, d in enumerate((0,) + OFFSETS):
-        if d:
-            landed(cg2, d)
-        g = (a1 - d + 4) % 4
-        block4 = pl.ds(pl.multiple_of(g * 4, 4), 4)
-        cxs.append(send(c4.at[block4], cx.at[block4], cx_send.at[d], cx_recv.at[d], partner))
         if n == 3:
             acc = red_s[0]
             for k in range(15):
@@ -430,6 +425,11 @@
                 rbs.append(
                     send(red_s.at[1], red_b.at[k - 1], rb_send.at[k - 1], rb_recv.at[k - 1], (o // 4, o % 4, z, c))
                 )
+        if d:
+            landed(cg2, d)
+        g = (a1 - d + 4) % 4
+        block4 = pl.ds(pl.multiple_of(g * 4, 4), 4)
+        cxs.append(send(c4.at[block4], cx.at[block4], cx_send.at[d], cx_recv.at[d], partner))
         rows_image(c4, 0, g)
         if n:
             cxs[n - 1].wait_recv()

time: 65.8 us -> 64.7 us (0.983)
  Pallas kernels: 63.4 us -> 62.3 us
    pallas_call x1, Pallas kernels: 63.4 us -> 62.3 us  [body(): pl.pallas_call(kernel, out_shape=(jax.ShapeDtypeStruct((128, D), BF16), j...]
where the time goes in v3:
time: 64.7 us; the launch traced here: 64.6 us
  Pallas kernels  62.3 us (96%)
  local copies, waits for them, and re-layouts  1.66 us (3%)
    pallas_call x1, Pallas kernels, body(): pl.pallas_call(kernel, out_shape=(jax.ShapeDtypeStruct((128, D), BF16), j...  62.3 us
    unnamed x2, local copies, waits for them, and re-layouts  1.66 us

profile of v3, /device:TPU:1, one launch (start us, length us, event | category | flops | bytes accessed | tf_op | source)
XLA Modules:
  0.0 64.6 jit_solution(12512705286669207988)
XLA Ops:
  0.6 62.3 %arnoldi.1 = (bf16[128,6144]{1,0:T(8,128)(2,1)S(1)}, f32[1,3]{1,0:T(1,128)S(1)}) custom-call(bf16[16,6144]{1,0:T(8,128)(2,1)} %tok_hbm.1, bf16[6144,128]{1,0:T(8,128)(2,1)} %wg_hbm.1, bf16[6144,128]{1,0:T(8,128)(2,1)} %wu_hbm.1, bf16[2,128,6144]{2,1,0:T(8,128)(2,1)} %basis_hbm.1, s32[2,256]{1,0:T(2,128)} %bitcast.7, f32[2,256]{1,0:T(2,128)} %bitcast.8, ...), custom_call_target="tpu_custom_call" | custom-call | tf_op jit(solution)/shard_map/arnoldi/pallas_call | solution.py:529
  63.0 1.1 %copy.12 = bf16[128,6144]{1,0:T(8,128)(2,1)} copy(bf16[128,6144]{1,0:T(8,128)(2,1)S(1)} %get-tuple-element.8) | data formatting | bytes 3145728
  64.1 0.5 copy.13

commit v4 on v3

--- a/solution.py
+++ b/solution.py
@@ -414,7 +414,7 @@
     cxs = []
     rbs = []
     for n, d in enumerate((0,) + OFFSETS):
-        if n == 3:
+        if n == 2:
             acc = red_s[0]
             for k in range(15):
                 ras[k].wait_recv()

time: 64.7 us -> 64.2 us (level)
  no operation moved by 1% of the time
where the time goes in v4:
time: 64.2 us; the launch traced here: 64.1 us
  Pallas kernels  61.8 us (96%)
  local copies, waits for them, and re-layouts  1.66 us (3%)
    pallas_call x1, Pallas kernels, body(): pl.pallas_call(kernel, out_shape=(jax.ShapeDtypeStruct((128, D), BF16), j...  61.8 us
    unnamed x2, local copies, waits for them, and re-layouts  1.66 us

profile of v4, /device:TPU:1, one launch (start us, length us, event | category | flops | bytes accessed | tf_op | source)
XLA Modules:
  0.0 64.1 jit_solution(14732222054737866458)
XLA Ops:
  0.6 61.8 %arnoldi.1 = (bf16[128,6144]{1,0:T(8,128)(2,1)S(1)}, f32[1,3]{1,0:T(1,128)S(1)}) custom-call(bf16[16,6144]{1,0:T(8,128)(2,1)} %tok_hbm.1, bf16[6144,128]{1,0:T(8,128)(2,1)} %wg_hbm.1, bf16[6144,128]{1,0:T(8,128)(2,1)} %wu_hbm.1, bf16[2,128,6144]{2,1,0:T(8,128)(2,1)} %basis_hbm.1, s32[2,256]{1,0:T(2,128)} %bitcast.7, f32[2,256]{1,0:T(2,128)} %bitcast.8, ...), custom_call_target="tpu_custom_call" | custom-call | tf_op jit(solution)/shard_map/arnoldi/pallas_call | solution.py:529
  62.5 1.1 %copy.12 = bf16[128,6144]{1,0:T(8,128)(2,1)} copy(bf16[128,6144]{1,0:T(8,128)(2,1)S(1)} %get-tuple-element.8) | data formatting | bytes 3145728
  63.6 0.5 copy.13

commit v5 on v4

--- a/solution.py
+++ b/solution.py
@@ -57,7 +57,7 @@
     routes, gates, rho, sigma, cols, tokv, wbuf, v0, v1, v0x, v1x, gm, gd, exf, exs, side_main, pre_s, pre_r, hid, hid_t,
     tb, r1, town, p2s, r2, tb0, r10, town0, held, sq_own, sq_out, sq_in, zs, rz0, zes, rz, amat, amat_h, rank_s, rho_s, c4, cx, cg, img,
     red_a, red_b, red_s,
-    loc_sem, core_send, core_recv, ag_send, ag_recv, rs_send, rs_recv, rt_send, rt_recv, sq_send, sq_recv, z_send, z_recv,
+    far_sem, loc_sem, core_send, core_recv, ag_send, ag_recv, rs_send, rs_recv, rt_send, rt_recv, sq_send, sq_recv, z_send, z_recv,
     cg_send, cg_recv, cx_send, cx_recv, ra_send, ra_recv, rb_send, rb_recv,
 ):
     y, x, z, c = [lax.axis_index(name) for name in AXES]
@@ -88,7 +88,8 @@
     barrier = pltpu.get_barrier_semaphore()
     greeted = [(y, x, z, 1 - c)]
     greeted += [((y + d) % 4, x, z, c) for d in OFFSETS] + [(y, (x + d) % 4, z, c) for d in OFFSETS]
-    greeted += [(y, x, (z + sg * d + 8) % 8, c) for d in (-1, 1, -2, 3)]
+    beside = [(y, x, (z + d) % 8, c) for d in (1, 7)]
+    greeted += beside
     for device in greeted:
         pl.semaphore_signal(barrier, inc=1, device_id=device, device_id_type=MESH)
 
@@ -145,7 +146,13 @@
         exs[r : r + 1, :] = picked[8:9, r * 384 : (r + 1) * 384]
     gm[m, :, HALF + SIDE : HALF + SIDE + 384] = exs[...].astype(BF16)
 
-    pl.semaphore_wait(barrier, 11)
+    pl.semaphore_wait(barrier, 9)
+
+    def hear(sem):
+        for device in beside:
+            pl.semaphore_signal(sem, inc=1, device_id=device, device_id_type=MESH)
+
+    hear(far_sem.at[0])
 
     def spread(ref, lap, s_sem, r_sem):
         index = a1 * 4 + (a2 + 4 - lap) % 4
@@ -194,11 +201,14 @@
     ]
 
     relay(first, second, gm, ag_send, ag_recv)
+    pl.semaphore_wait(far_sem.at[0], 2)
+    hear(far_sem.at[1])
 
     for d in OFFSETS:
         landed(second, d)
     for copy in loads[1:]:
         copy.wait()
+    pl.semaphore_wait(far_sem.at[1], 2)
     for copy in core:
         copy.wait_recv()
 
@@ -512,6 +522,7 @@
         pltpu.VMEM((15, 8, 128), F32),
         pltpu.VMEM((15, 8, 128), F32),
         pltpu.VMEM((2, 8, 128), F32),
+        pltpu.SemaphoreType.REGULAR((2,)),
         dma((11,)),
         dma((5,)), dma((5,)),
         dma((5, 3)), dma((5, 3)),

time: 64.2 us -> 64.4 us (level)
  no operation moved by 1% of the time
where the time goes in v5:
time: 64.4 us; the launch traced here: 64.3 us
  Pallas kernels  62 us (96%)
  local copies, waits for them, and re-layouts  1.66 us (3%)
    pallas_call x1, Pallas kernels, body(): pl.pallas_call(kernel, out_shape=(jax.ShapeDtypeStruct((128, D), BF16), j...  62 us
    unnamed x2, local copies, waits for them, and re-layouts  1.66 us

profile of v5, /device:TPU:1, one launch (start us, length us, event | category | flops | bytes accessed | tf_op | source)
XLA Modules:
  0.0 64.3 jit_solution(14585951246219774508)
XLA Ops:
  0.6 62.0 %arnoldi.1 = (bf16[128,6144]{1,0:T(8,128)(2,1)S(1)}, f32[1,3]{1,0:T(1,128)S(1)}) custom-call(bf16[16,6144]{1,0:T(8,128)(2,1)} %tok_hbm.1, bf16[6144,128]{1,0:T(8,128)(2,1)} %wg_hbm.1, bf16[6144,128]{1,0:T(8,128)(2,1)} %wu_hbm.1, bf16[2,128,6144]{2,1,0:T(8,128)(2,1)} %basis_hbm.1, s32[2,256]{1,0:T(2,128)} %bitcast.7, f32[2,256]{1,0:T(2,128)} %bitcast.8, ...), custom_call_target="tpu_custom_call" | custom-call | tf_op jit(solution)/shard_map/arnoldi/pallas_call | solution.py:540
  62.6 1.1 %copy.12 = bf16[128,6144]{1,0:T(8,128)(2,1)} copy(bf16[128,6144]{1,0:T(8,128)(2,1)S(1)} %get-tuple-element.8) | data formatting | bytes 3145728
  63.8 0.5 copy.13
